TPU v7x, 256 devices: a whole 4x4x8 slice. The times are simulated.
256 devices in a mesh: gx: 32 (over y, z), gy: 8 (over x, core).
Axes of the slice: x: 4, y: 4, z: 8, core: 2. Of those that a mesh axis runs over, the one named last changes fastest.
Arguments:
- densities: bfloat16 [24576, 32, 128], P(('gx', 'gy')), may hold values from -6 to 6
- geometry: float32 [24576, 7, 128], P(('gx', 'gy')), as said below
- near_ids: int32 [24576, 8], P(('gx', 'gy')), may hold values from 0 to 24575, as said below
- basis_in: bfloat16 [24576, 64, 128], P(('gx', 'gy')), may hold values from -0.5 to 0.5
- basis_out: bfloat16 [24576, 64, 128], P(('gx', 'gy')), may hold values from -0.75 to 0.75
- leaf_up: bfloat16 [24576, 64, 64], P(('gx', 'gy')), may hold values from -0.078125 to 0.078125
- leaf_down: bfloat16 [24576, 64, 64], P(('gx', 'gy')), may hold values from -0.75 to 0.75
- leaf_coupling: bfloat16 [24576, 6, 64, 64], P(('gx', 'gy')), may hold values from -0.3125 to 0.3125
- leaf_far: int32 [24576, 6], P(('gx', 'gy')), may hold values from 0 to 24575, as said below
- leaf_count: int32 [24576], P(('gx', 'gy')), may hold values from 1 to 6, as said below
- cluster_up: bfloat16 [256, 64, 64], P(('gx', 'gy')), may hold values from -0.25 to 0.25
- cluster_down: bfloat16 [256, 64, 64], P(('gx', 'gy')), may hold values from -0.75 to 0.75
- cluster_coupling: bfloat16 [256, 6, 64, 64], P(('gx', 'gy')), may hold values from -0.3125 to 0.3125
- cluster_far: int32 [256, 6], P(('gx', 'gy')), may hold values from 0 to 255, as said below
- group_up: bfloat16 [32, 64, 64], replicated, may hold values from -0.375 to 0.375
- group_down: bfloat16 [32, 64, 64], P('gx'), may hold values from -0.75 to 0.75
- group_coupling: bfloat16 [32, 6, 64, 64], P('gx'), may hold values from -0.3125 to 0.3125
- group_far: int32 [32, 6], P('gx'), may hold values from 0 to 31, as said below
- root_coupling: bfloat16 [8, 8, 64, 64], replicated, may hold values from -0.25 to 0.25
Outputs:
- potential: float32 [24576, 32, 128], P(('gx', 'gy'))
Inputs may be any that keep to these rules, and one draw needn't show every extreme that they name: `near_ids`: row l names 8 different leaves of a window of 9 consecutive leaves that contains l, centred on l where the ends allow. `leaf_far`: row l names 6 different leaves held by l's device or its two neighbours in leaf order, none within 4 leaves of l; only the first leaf_count[l] entries are used. `leaf_count`: every device holds a leaf with 6. `cluster_far`: row u names 6 different level-two clusters other than u, of u's group or the two groups beside it. `group_far`: row g names 6 different level-one clusters other than g. `geometry`: rows 0 to 2 hold a panel's centre, rows 3 to 5 its unit normal, row 6 its area, from 0.25 to 2.
All inputs are finite; a program needn't handle non-finite values.
Results may differ from a plain program's by a relative error of at most 0.012.
Values may be sent and summed in bfloat16 or wider, within the bound.
A program may use at most 128 MiB of HBM per device.

v0:
```python
import math
import jax
import jax.numpy as jnp
from jax import lax
from jax.sharding import PartitionSpec as P

REACH = 4
BRANCH = 4
four_pi = 4.0 * math.pi
leaf_block = 8


def padded(cells, sides, width):
    for axis, dim in sides:
        count = lax.axis_size(axis)
        ends = count - 1
        head = lax.slice_in_dim(cells, 0, width, axis=dim)
        tail = lax.slice_in_dim(cells, cells.shape[dim] - width, cells.shape[dim], axis=dim)
        cells = jnp.concatenate(
            [
                lax.ppermute(tail, axis, [(i, (i + 1) % count) for i in range(ends)]),
                cells,
                lax.ppermute(head, axis, [((i + 1) % count, i) for i in range(ends)]),
            ],
            axis=dim,
        )
    return cells


def near_kernel(target, source):
    offsets = [
        target[:, coord_id, :, None, None] - source[:, None, :, coord_id, :]
        for coord_id in range(3)
    ]
    distance = offsets[0] * offsets[0] + offsets[1] * offsets[1] + offsets[2] * offsets[2]
    facing = (
        source[:, None, :, 3, :] * offsets[0]
        + source[:, None, :, 4, :] * offsets[1]
        + source[:, None, :, 5, :] * offsets[2]
    )
    panel_area = source[:, None, :, 6, :]
    spread = distance + panel_area
    return panel_area * facing / (four_pi * spread * jnp.sqrt(spread))


def on_device(
    densities,
    geometry,
    near_ids,
    basis_in,
    basis_out,
    leaf_up,
    leaf_down,
    leaf_coupling,
    leaf_far,
    leaf_count,
    cluster_up,
    cluster_down,
    cluster_coupling,
    cluster_far,
    group_up,
    group_down,
    group_coupling,
    group_far,
    root_coupling,
):
    wide = jnp.float32
    narrow = jnp.bfloat16
    leaves = densities.shape[0]
    coeff_order = basis_in.shape[1]
    columns = densities.shape[1]
    flat = coeff_order * columns
    first_leaf = lax.axis_index(("gx", "gy")) * leaves
    gx_index = lax.axis_index("gx")
    group_size = lax.axis_size("gy")
    groups = lax.axis_size("gx")
    leaf_coeffs = jnp.einsum(
        "lkm,lrm->lkr", basis_in, densities, preferred_element_type=wide
    ).astype(narrow)
    mid_coeffs = jnp.einsum(
        "lik,lkr->ir", leaf_up, leaf_coeffs, preferred_element_type=wide
    ).astype(narrow)
    mid_term = jnp.dot(cluster_up[0], mid_coeffs, preferred_element_type=wide).reshape(1, flat)
    mid_flat = mid_coeffs.reshape(1, flat)
    siblings = lax.all_gather(mid_flat, "gy", axis=0, tiled=True)
    group_sum = lax.psum(mid_term, "gy")
    nearby = padded(siblings, (("gx", 0),), group_size)
    mid_picked = jnp.take(nearby, cluster_far[0] - (gx_index - 1) * group_size, axis=0)
    top_coeffs = lax.all_gather(group_sum.astype(narrow), "gx", axis=0, tiled=True)
    top_block = top_coeffs.reshape(groups, coeff_order, columns)
    root_terms = jnp.einsum("gik,gkr->gir", group_up, top_block, preferred_element_type=wide)
    root_coeffs = jnp.sum(
        root_terms.reshape(groups // BRANCH, BRANCH, coeff_order, columns), axis=1
    ).astype(narrow)
    root_row = lax.dynamic_index_in_dim(root_coupling, gx_index // BRANCH, 0, keepdims=False)
    root_field = jnp.einsum(
        "sik,skr->ir", root_row, root_coeffs, preferred_element_type=wide
    ).astype(narrow)
    top_picked = jnp.take(top_block, group_far[0], axis=0)
    top_field = (
        jnp.einsum("fik,fkr->ir", group_coupling[0], top_picked, preferred_element_type=wide)
        + jnp.dot(group_down[0], root_field, preferred_element_type=wide)
    ).astype(narrow)
    mid_block = mid_picked.reshape(-1, coeff_order, columns)
    mid_field = (
        jnp.einsum("fik,fkr->ir", cluster_coupling[0], mid_block, preferred_element_type=wide)
        + jnp.dot(cluster_down[0], top_field, preferred_element_type=wide)
    ).astype(narrow)
    coeff_rim = padded(leaf_coeffs.reshape(leaves, flat), ((("gx", "gy"), 0),), leaves)
    picked = jnp.take(coeff_rim, leaf_far - (first_leaf - leaves), axis=0).reshape(
        leaves, -1, coeff_order, columns
    )
    live_mask = (lax.broadcasted_iota(jnp.int32, leaf_far.shape, 1) < leaf_count[:, None]).astype(
        narrow
    )
    picked = picked * live_mask[:, :, None, None]
    leaf_field = (
        jnp.einsum("lfik,lfkr->lir", leaf_coupling, picked, preferred_element_type=wide)
        + jnp.einsum("lik,kr->lir", leaf_down, mid_field, preferred_element_type=wide)
    ).astype(narrow)
    far_part = jnp.einsum("lkr,lkm->lrm", leaf_field, basis_out, preferred_element_type=wide)
    values_rim = padded(densities, ((("gx", "gy"), 0),), REACH)
    shape_rim = padded(geometry, ((("gx", "gy"), 0),), REACH)
    near_local = near_ids - (first_leaf - REACH)

    def near_block(pieces):
        target, indices = pieces
        source = jnp.take(shape_rim, indices, axis=0)
        values = jnp.take(values_rim, indices, axis=0)
        kernel = near_kernel(target, source).astype(narrow)
        return jnp.einsum("bmnj,bnrj->brm", kernel, values, preferred_element_type=wide)

    near_part = lax.map(
        near_block,
        (
            geometry.reshape(leaves // leaf_block, leaf_block, 7, -1),
            near_local.reshape(leaves // leaf_block, leaf_block, -1),
        ),
    )
    return far_part + near_part.reshape(far_part.shape)


def solution(mesh):
    return jax.shard_map(
        on_device,
        mesh=mesh,
        in_specs=(
            P(("gx", "gy"), None, None),
            P(("gx", "gy"), None, None),
            P(("gx", "gy"), None),
            P(("gx", "gy"), None, None),
            P(("gx", "gy"), None, None),
            P(("gx", "gy"), None, None),
            P(("gx", "gy"), None, None),
            P(("gx", "gy"), None, None, None),
            P(("gx", "gy"), None),
            P(("gx", "gy")),
            P(("gx", "gy"), None, None),
            P(("gx", "gy"), None, None),
            P(("gx", "gy"), None, None, None),
            P(("gx", "gy"), None),
            P(),
            P("gx", None, None),
            P("gx", None, None, None),
            P("gx", None),
            P(),
        ),
        out_specs=P(("gx", "gy"), None, None),
        check_vma=False,
    )
```

profile of v0, /device:TPU:8, one launch (start us, length us, event | category | flops | bytes accessed | tf_op | source)
XLA Modules:
  0.0 328.0 jit_solution(2928487035204301218)
XLA Ops:
  0.0 2.6 convolution_convert_fusion
  2.6 1.3 copy.65
  4.0 1.0 copy.66
  4.9 9.3 %collective-permute-start.1 = (bf16[96,2048]{1,0:T(8,128)(2,1)}, bf16[96,2048]{1,0:T(8,128)(2,1)}, u32[]{:S(2)}, u32[]{:S(2)}) collective-permute-start(bf16[96,2048]{1,0:T(8,128)(2,1)} %copy.66), channel_id=1, source_target_pairs={{1,0},{2,1},{3,2},{4,3},{5,4},{6,5},{7,6},{8,7},{9,8},{10,9},{11,1... | collective-permute-start | bytes 1179656 | tf_op jit(solution)/shard_map/ppermute | solution.py:23
  14.2 1.9 collective-permute-start
  16.2 1.2 copy.80
  17.4 1.9 collective-permute-start.6
  19.3 8.0 %collective-permute-start.7 = (f32[4,7,128]{2,1,0:T(8,128)S(1)}, f32[4,7,128]{2,1,0:T(8,128)S(1)}, u32[]{:S(2)}, u32[]{:S(2)}) collective-permute-start(f32[4,7,128]{2,1,0:T(8,128)S(1)} %get-tuple-element.83), channel_id=1, source_target_pairs={{1,0},{2,1},{3,2},{4,3},{5,4},{6,5},{7,6},{8,7},{9,8},{10,9},{11,1... | collective-permute-start | bytes 43016 | tf_op jit(solution)/shard_map/ppermute | solution.py:23
  27.3 4.0 %copy.72 = bf16[96,64,64]{2,1,0:T(8,128)(2,1)} copy(bf16[96,64,64]{0,2,1:T(8,128)(2,1)} %param.26) | data formatting | bytes 1572864 | tf_op args[5]
  31.4 2.0 fusion.35
  33.5 12.8 %all-gather = bf16[8,1,2048]{2,1,0:T(2,128)(2,1)S(1)} all-gather(bf16[1,1,2048]{2,1,0:T(2,128)(2,1)S(1)} %reshape.240), channel_id=1, replica_groups=mesh['gx'=32,'gy'=8] {'gy'}, dimensions={0}, use_global_device_ids=true | all-gather | bytes 36864 | tf_op jit(solution)/shard_map/all_gather | solution.py:85
  46.3 1.9 collective-permute-start.3
  48.4 0.8 fusion.62
  50.4 24.5 %psum.7 = bf16[1,2048]{1,0:T(2,128)(2,1)S(1)} all-reduce(f32[1,2048]{1,0:T(1,128)S(1)} %reshape.189), channel_id=1, replica_groups=mesh['gx'=32,'gy'=8] {'gy'}, use_global_device_ids=true, to_apply=%region_0.0 | all-reduce | flops 2048 | bytes 12288 | tf_op jit(solution)/shard_map/psum | solution.py:86
  74.9 48.0 %all-gather.1 = bf16[32,1,2048]{2,1,0:T(2,128)(2,1)S(1)} all-gather(bf16[1,1,2048]{2,1,0:T(2,128)(2,1)S(1)} %bitcast.169), channel_id=1, replica_groups=mesh['gx'=32,'gy'=8] {'gx'}, dimensions={0}, use_global_device_ids=true | all-gather | bytes 135168 | tf_op jit(solution)/shard_map/all_gather | solution.py:89
  125.1 1.1 convolution_bitcast_fusion.1
  126.2 1.8 fusion.33
  129.4 4.0 %copy.78 = bf16[96,64,64]{2,1,0:T(8,128)(2,1)} copy(bf16[96,64,64]{0,2,1:T(8,128)(2,1)} %param.27) | data formatting | bytes 1572864 | tf_op args[6]
  133.4 16.1 %copy.71 = bf16[96,6,64,64]{3,2,1,0:T(8,128)(2,1)} copy(bf16[96,6,64,64]{0,3,2,1:T(8,128)(2,1)} %param.28) | data formatting | bytes 9437184 | tf_op args[7]
  149.5 2.4 collective-permute-start.2
  152.0 1.9 collective-permute-start.4
  154.0 8.0 %collective-permute-start.5 = (bf16[4,32,128]{2,1,0:T(8,128)(2,1)S(1)}, bf16[4,32,128]{2,1,0:T(8,128)(2,1)S(1)}, u32[]{:S(2)}, u32[]{:S(2)}) collective-permute-start(bf16[4,32,128]{2,1,0:T(8,128)(2,1)S(1)} %get-tuple-element.81), channel_id=1, source_target_pairs={{1,0},{2,1},{3,2},{4,3},{5,4},{6,5},{7,6},{8,7},{9,8},{10,9},{11,1... | collective-permute-start | bytes 98312 | tf_op jit(solution)/shard_map/ppermute | solution.py:23
  163.5 1.2 pad_maximum_fusion.1
  164.7 130.7 %while.10 = (s32[]{:T(128)}, f32[12,8,32,128]{3,2,1,0:T(8,128)}, s32[12,8,8]{2,1,0:T(8,128)}, bf16[104,32,128]{2,1,0:T(8,128)(2,1)S(1)}, f32[104,7,128]{2,1,0:T(...) while((s32[]{:T(128)}, f32[12,8,32,128]{3,2,1,0:T(8,128)}, s32[12,8,8]{2,1,0:T(8,128)}, ...), condition=%wide.region_3.4_spmd, body=%wide.region_2.3_spmd.sunk | while | flops 87352896 | bytes 3410213 | solution.py:133
  166.2 0.8 dynamic-slice_bitcast_fusion.2
  168.3 0.8 fusion.83
  169.7 5.9 %fusion.84 = f32[12,8,32,128]{3,2,1,0:T(8,128)} fusion(f32[12,8,32,128]{3,2,1,0:T(8,128)} %get-tuple-element.149, s32[]{:T(128)S(6)} %copy.97, f32[8,8,128]{2,1,0:T(8,128)S(1)} %bitcast.159, f32[8,128]{1,0:T(8,128)} %get-tuple-element.132, f32[8,8,128]{2,1,0:T(8,128)S(1)} %bitcast.160, f32[8,8,128]{2,1,0:T(8,128)S(1)} %bitcast.161, ...), kind=kOutput, calls=%fused_computation.21.clone.1 | convolution fusion | flops 87293952 | bytes 897092 | tf_op jit(solution)/shard_map/while/body/eval_jaxpr/bmnj,bnrj->brm/dot_general | solution.py:131
  177.1 0.8 dynamic-slice_bitcast_fusion.2
  179.2 0.8 fusion.83
  180.6 5.9 %fusion.84 = f32[12,8,32,128]{3,2,1,0:T(8,128)} fusion(f32[12,8,32,128]{3,2,1,0:T(8,128)} %get-tuple-element.149, s32[]{:T(128)S(6)} %copy.97, f32[8,8,128]{2,1,0:T(8,128)S(1)} %bitcast.159, f32[8,128]{1,0:T(8,128)} %get-tuple-element.132, f32[8,8,128]{2,1,0:T(8,128)S(1)} %bitcast.160, f32[8,8,128]{2,1,0:T(8,128)S(1)} %bitcast.161, ...), kind=kOutput, calls=%fused_computation.21.clone.1 | convolution fusion | flops 87293952 | bytes 897092 | tf_op jit(solution)/shard_map/while/body/eval_jaxpr/bmnj,bnrj->brm/dot_general | solution.py:131
  188.0 0.8 dynamic-slice_bitcast_fusion.2
  190.1 0.8 fusion.83
  191.5 5.9 %fusion.84 = f32[12,8,32,128]{3,2,1,0:T(8,128)} fusion(f32[12,8,32,128]{3,2,1,0:T(8,128)} %get-tuple-element.149, s32[]{:T(128)S(6)} %copy.97, f32[8,8,128]{2,1,0:T(8,128)S(1)} %bitcast.159, f32[8,128]{1,0:T(8,128)} %get-tuple-element.132, f32[8,8,128]{2,1,0:T(8,128)S(1)} %bitcast.160, f32[8,8,128]{2,1,0:T(8,128)S(1)} %bitcast.161, ...), kind=kOutput, calls=%fused_computation.21.clone.1 | convolution fusion | flops 87293952 | bytes 897092 | tf_op jit(solution)/shard_map/while/body/eval_jaxpr/bmnj,bnrj->brm/dot_general | solution.py:131
  198.9 0.8 dynamic-slice_bitcast_fusion.2
  201.0 0.8 fusion.83
  202.4 5.9 %fusion.84 = f32[12,8,32,128]{3,2,1,0:T(8,128)} fusion(f32[12,8,32,128]{3,2,1,0:T(8,128)} %get-tuple-element.149, s32[]{:T(128)S(6)} %copy.97, f32[8,8,128]{2,1,0:T(8,128)S(1)} %bitcast.159, f32[8,128]{1,0:T(8,128)} %get-tuple-element.132, f32[8,8,128]{2,1,0:T(8,128)S(1)} %bitcast.160, f32[8,8,128]{2,1,0:T(8,128)S(1)} %bitcast.161, ...), kind=kOutput, calls=%fused_computation.21.clone.1 | convolution fusion | flops 87293952 | bytes 897092 | tf_op jit(solution)/shard_map/while/body/eval_jaxpr/bmnj,bnrj->brm/dot_general | solution.py:131
  209.8 0.8 dynamic-slice_bitcast_fusion.2
  211.9 0.8 fusion.83
  213.3 5.9 %fusion.84 = f32[12,8,32,128]{3,2,1,0:T(8,128)} fusion(f32[12,8,32,128]{3,2,1,0:T(8,128)} %get-tuple-element.149, s32[]{:T(128)S(6)} %copy.97, f32[8,8,128]{2,1,0:T(8,128)S(1)} %bitcast.159, f32[8,128]{1,0:T(8,128)} %get-tuple-element.132, f32[8,8,128]{2,1,0:T(8,128)S(1)} %bitcast.160, f32[8,8,128]{2,1,0:T(8,128)S(1)} %bitcast.161, ...), kind=kOutput, calls=%fused_computation.21.clone.1 | convolution fusion | flops 87293952 | bytes 897092 | tf_op jit(solution)/shard_map/while/body/eval_jaxpr/bmnj,bnrj->brm/dot_general | solution.py:131
  220.6 0.8 dynamic-slice_bitcast_fusion.2
  222.8 0.8 fusion.83
  224.2 5.9 %fusion.84 = f32[12,8,32,128]{3,2,1,0:T(8,128)} fusion(f32[12,8,32,128]{3,2,1,0:T(8,128)} %get-tuple-element.149, s32[]{:T(128)S(6)} %copy.97, f32[8,8,128]{2,1,0:T(8,128)S(1)} %bitcast.159, f32[8,128]{1,0:T(8,128)} %get-tuple-element.132, f32[8,8,128]{2,1,0:T(8,128)S(1)} %bitcast.160, f32[8,8,128]{2,1,0:T(8,128)S(1)} %bitcast.161, ...), kind=kOutput, calls=%fused_computation.21.clone.1 | convolution fusion | flops 87293952 | bytes 897092 | tf_op jit(solution)/shard_map/while/body/eval_jaxpr/bmnj,bnrj->brm/dot_general | solution.py:131
  231.5 0.8 dynamic-slice_bitcast_fusion.2
  233.7 0.8 fusion.83
  235.1 5.9 %fusion.84 = f32[12,8,32,128]{3,2,1,0:T(8,128)} fusion(f32[12,8,32,128]{3,2,1,0:T(8,128)} %get-tuple-element.149, s32[]{:T(128)S(6)} %copy.97, f32[8,8,128]{2,1,0:T(8,128)S(1)} %bitcast.159, f32[8,128]{1,0:T(8,128)} %get-tuple-element.132, f32[8,8,128]{2,1,0:T(8,128)S(1)} %bitcast.160, f32[8,8,128]{2,1,0:T(8,128)S(1)} %bitcast.161, ...), kind=kOutput, calls=%fused_computation.21.clone.1 | convolution fusion | flops 87293952 | bytes 897092 | tf_op jit(solution)/shard_map/while/body/eval_jaxpr/bmnj,bnrj->brm/dot_general | solution.py:131
  242.4 0.8 dynamic-slice_bitcast_fusion.2
  244.6 0.8 fusion.83
  246.0 5.9 %fusion.84 = f32[12,8,32,128]{3,2,1,0:T(8,128)} fusion(f32[12,8,32,128]{3,2,1,0:T(8,128)} %get-tuple-element.149, s32[]{:T(128)S(6)} %copy.97, f32[8,8,128]{2,1,0:T(8,128)S(1)} %bitcast.159, f32[8,128]{1,0:T(8,128)} %get-tuple-element.132, f32[8,8,128]{2,1,0:T(8,128)S(1)} %bitcast.160, f32[8,8,128]{2,1,0:T(8,128)S(1)} %bitcast.161, ...), kind=kOutput, calls=%fused_computation.21.clone.1 | convolution fusion | flops 87293952 | bytes 897092 | tf_op jit(solution)/shard_map/while/body/eval_jaxpr/bmnj,bnrj->brm/dot_general | solution.py:131
  255.4 0.8 fusion.83
  256.9 5.9 %fusion.84 = f32[12,8,32,128]{3,2,1,0:T(8,128)} fusion(f32[12,8,32,128]{3,2,1,0:T(8,128)} %get-tuple-element.149, s32[]{:T(128)S(6)} %copy.97, f32[8,8,128]{2,1,0:T(8,128)S(1)} %bitcast.159, f32[8,128]{1,0:T(8,128)} %get-tuple-element.132, f32[8,8,128]{2,1,0:T(8,128)S(1)} %bitcast.160, f32[8,8,128]{2,1,0:T(8,128)S(1)} %bitcast.161, ...), kind=kOutput, calls=%fused_computation.21.clone.1 | convolution fusion | flops 87293952 | bytes 897092 | tf_op jit(solution)/shard_map/while/body/eval_jaxpr/bmnj,bnrj->brm/dot_general | solution.py:131
  264.2 0.8 dynamic-slice_bitcast_fusion.2
  266.3 0.8 fusion.83
  267.8 5.9 %fusion.84 = f32[12,8,32,128]{3,2,1,0:T(8,128)} fusion(f32[12,8,32,128]{3,2,1,0:T(8,128)} %get-tuple-element.149, s32[]{:T(128)S(6)} %copy.97, f32[8,8,128]{2,1,0:T(8,128)S(1)} %bitcast.159, f32[8,128]{1,0:T(8,128)} %get-tuple-element.132, f32[8,8,128]{2,1,0:T(8,128)S(1)} %bitcast.160, f32[8,8,128]{2,1,0:T(8,128)S(1)} %bitcast.161, ...), kind=kOutput, calls=%fused_computation.21.clone.1 | convolution fusion | flops 87293952 | bytes 897092 | tf_op jit(solution)/shard_map/while/body/eval_jaxpr/bmnj,bnrj->brm/dot_general | solution.py:131
  275.1 0.8 dynamic-slice_bitcast_fusion.2
  277.2 0.8 fusion.83
  278.7 5.9 %fusion.84 = f32[12,8,32,128]{3,2,1,0:T(8,128)} fusion(f32[12,8,32,128]{3,2,1,0:T(8,128)} %get-tuple-element.149, s32[]{:T(128)S(6)} %copy.97, f32[8,8,128]{2,1,0:T(8,128)S(1)} %bitcast.159, f32[8,128]{1,0:T(8,128)} %get-tuple-element.132, f32[8,8,128]{2,1,0:T(8,128)S(1)} %bitcast.160, f32[8,8,128]{2,1,0:T(8,128)S(1)} %bitcast.161, ...), kind=kOutput, calls=%fused_computation.21.clone.1 | convolution fusion | flops 87293952 | bytes 897092 | tf_op jit(solution)/shard_map/while/body/eval_jaxpr/bmnj,bnrj->brm/dot_general | solution.py:131
  288.1 0.8 fusion.83
  289.6 5.9 %fusion.84 = f32[12,8,32,128]{3,2,1,0:T(8,128)} fusion(f32[12,8,32,128]{3,2,1,0:T(8,128)} %get-tuple-element.149, s32[]{:T(128)S(6)} %copy.97, f32[8,8,128]{2,1,0:T(8,128)S(1)} %bitcast.159, f32[8,128]{1,0:T(8,128)} %get-tuple-element.132, f32[8,8,128]{2,1,0:T(8,128)S(1)} %bitcast.160, f32[8,8,128]{2,1,0:T(8,128)S(1)} %bitcast.161, ...), kind=kOutput, calls=%fused_computation.21.clone.1 | convolution fusion | flops 87293952 | bytes 897092 | tf_op jit(solution)/shard_map/while/body/eval_jaxpr/bmnj,bnrj->brm/dot_general | solution.py:131
  295.4 1.1 convolution_bitcast_fusion.3
  296.5 4.3 %fusion.37 = f32[32,96,64]{2,0,1:T(8,128)} fusion(bf16[96,64,64]{2,1,0:T(8,128)(2,1)} %copy.78, f32[32,64]{1,0:T(8,128)S(1)} %convolution_bitcast_fusion.3, bf16[32,64]{1,0:T(8,128)(2,1)} %fusion.33, bf16[1,64,64]{2,1,0:T(8,128)(2,1)} %param.32), kind=kOutput, calls=%fused_computation.60 | convolution fusion | flops 25432064 | bytes 1593344 | tf_op jit(solution)/shard_map/lik,kr->lir/dot_general | solution.py:119
  300.8 1.3 pad_maximum_fusion
  302.1 4.0 %gather_fusion.2 = bf16[576,2048]{1,0:T(8,128)(2,1)} fusion(bf16[288,2048]{1,0:T(8,128)(2,1)S(1)} %pad_maximum_fusion, s32[1024]{0:T(1024)S(1)} %pad_clamp_fusion.3), kind=kCustom, calls=%fused_computation.2 | custom fusion | bytes 4720896 | tf_op jit(solution)/shard_map/jit(_take)/gather | solution.py:110
  306.1 11.7 %gather.23 = bf16[96,6,64,32]{3,2,1,0:T(8,128)(2,1)} reshape(bf16[576,2048]{1,0:T(8,128)(2,1)} %gather_fusion.2) | data formatting | bytes 4718592 | tf_op jit(solution)/shard_map/jit(_take)/gather | solution.py:110
  317.8 10.3 %bitcast_add_fusion.1 = f32[96,32,128]{2,1,0:T(8,128)} fusion(f32[12,8,32,128]{3,2,1,0:T(8,128)} %get-tuple-element.37, bf16[96,64,128]{2,1,0:T(8,128)(2,1)S(1)} %copy-done, f32[32,96,64]{2,0,1:T(8,128)S(1)} %copy-done.1, bf16[96,6,64,64]{3,2,1,0:T(8,128)(2,1)} %copy.71, bf16[96,6,64,32]{3,2,1,0:T(8,128)(2,1)} %gather.23, pred[96,6]{1,0:T(8,128)(4,1)S(1)} %copy-done.6, ...), kind=kOutput, calls=%fused_computation.44 | convolution fusion | flops 204472320 | bytes 12584640 | tf_op jit(solution)/shard_map/lkr,lkm->lrm/dot_general | solution.py:121
  (161 shorter events, 49.6 us)
Async XLA Ops:
  0.0 317.8 %copy-start = (bf16[96,64,128]{2,1,0:T(8,128)(2,1)S(1)}, bf16[96,64,128]{2,1,0:T(8,128)(2,1)}, u32[]{:S(2)}) copy-start(bf16[96,64,128]{2,1,0:T(8,128)(2,1)} %param.25) | copy-start | bytes 4718596
  4.9 295.9 %collective-permute-start.1 = (bf16[96,2048]{1,0:T(8,128)(2,1)}, bf16[96,2048]{1,0:T(8,128)(2,1)}, u32[]{:S(2)}, u32[]{:S(2)}) collective-permute-start(bf16[96,2048]{1,0:T(8,128)(2,1)} %copy.66), channel_id=1, source_target_pairs={{1,0},{2,1},{3,2},{4,3},{5,4},{6,5},{7,6},{8,7},{9,8},{10,9},{11,1... | collective-permute-start | bytes 1179656 | tf_op jit(solution)/shard_map/ppermute | solution.py:23
  14.2 286.6 %collective-permute-start = (bf16[96,2048]{1,0:T(8,128)(2,1)}, bf16[96,2048]{1,0:T(8,128)(2,1)}, u32[]{:S(2)}, u32[]{:S(2)}) collective-permute-start(bf16[96,2048]{1,0:T(8,128)(2,1)} %copy.66), channel_id=1, source_target_pairs={{0,1},{1,2},{2,3},{3,4},{4,5},{5,6},{6,7},{7,8},{8,9},{9,10},{10,1... | collective-permute-start | bytes 1179656 | tf_op jit(solution)/shard_map/ppermute | solution.py:21
  17.4 132.2 %collective-permute-start.6 = (f32[4,7,128]{2,1,0:T(8,128)S(1)}, f32[4,7,128]{2,1,0:T(8,128)S(1)}, u32[]{:S(2)}, u32[]{:S(2)}) collective-permute-start(f32[4,7,128]{2,1,0:T(8,128)S(1)} %get-tuple-element.82), channel_id=1, source_target_pairs={{0,1},{1,2},{2,3},{3,4},{4,5},{5,6},{6,7},{7,8},{8,9},{9,10},{10,1... | collective-permute-start | bytes 43016 | tf_op jit(solution)/shard_map/ppermute | solution.py:21
  19.3 29.0 %copy-start.10 = (s32[1,6]{1,0:T(1,128)S(1)}, s32[1,6]{1,0:T(1,128)}, u32[]{:S(2)}) copy-start(s32[1,6]{1,0:T(1,128)} %param.34) | copy-start | bytes 76
  19.3 29.0 %copy-start.11 = (s32[1,6]{1,0:T(1,128)S(1)}, s32[1,6]{1,0:T(1,128)}, u32[]{:S(2)}) copy-start(s32[1,6]{1,0:T(1,128)} %param.38) | copy-start | bytes 76
  19.3 29.8 %copy-start.9 = (s32[96]{0:T(128)S(1)}, s32[96]{0:T(128)}, u32[]{:S(2)}) copy-start(s32[96]{0:T(128)} %param.30) | copy-start | bytes 1156
  19.3 30.5 %copy-start.7 = (s32[96,6]{0,1:T(8,128)S(1)}, s32[96,6]{0,1:T(8,128)}, u32[]{:S(2)}) copy-start(s32[96,6]{0,1:T(8,128)} %param.29) | copy-start | bytes 6916
  19.3 30.8 %copy-start.4 = (bf16[1,64,64]{2,1,0:T(8,128)(2,1)S(1)}, bf16[1,64,64]{2,1,0:T(8,128)(2,1)}, u32[]{:S(2)}) copy-start(bf16[1,64,64]{2,1,0:T(8,128)(2,1)} %param.31) | copy-start | bytes 24580
  19.3 132.6 %collective-permute-start.7 = (f32[4,7,128]{2,1,0:T(8,128)S(1)}, f32[4,7,128]{2,1,0:T(8,128)S(1)}, u32[]{:S(2)}, u32[]{:S(2)}) collective-permute-start(f32[4,7,128]{2,1,0:T(8,128)S(1)} %get-tuple-element.83), channel_id=1, source_target_pairs={{1,0},{2,1},{3,2},{4,3},{5,4},{6,5},{7,6},{8,7},{9,8},{10,9},{11,1... | collective-permute-start | bytes 43016 | tf_op jit(solution)/shard_map/ppermute | solution.py:23
  31.4 92.7 %copy-start.2 = (bf16[32,64,64]{2,1,0:T(8,128)(2,1)S(1)}, bf16[32,64,64]{2,1,0:T(8,128)(2,1)}, u32[]{:S(2)}) copy-start(bf16[32,64,64]{2,1,0:T(8,128)(2,1)} %param.35) | copy-start | bytes 786436
  31.4 93.7 %copy-start.8 = (s32[96,8]{0,1:T(8,128)S(1)}, s32[96,8]{0,1:T(8,128)}, u32[]{:S(2)}) copy-start(s32[96,8]{0,1:T(8,128)} %param.23) | copy-start | bytes 9220
  33.3 92.9 %copy-start.5 = (bf16[1,64,64]{2,1,0:T(8,128)(2,1)S(1)}, bf16[1,64,64]{2,1,0:T(8,128)(2,1)}, u32[]{:S(2)}) copy-start(bf16[1,64,64]{2,1,0:T(8,128)(2,1)} %param.36) | copy-start | bytes 24580
  46.3 107.6 %collective-permute-start.3 = (bf16[8,2048]{1,0:T(8,128)(2,1)S(1)}, bf16[8,2048]{1,0:T(8,128)(2,1)S(1)}, u32[]{:S(2)}, u32[]{:S(2)}) collective-permute-start(bf16[8,2048]{1,0:T(8,128)(2,1)S(1)} %bitcast.165), channel_id=1, source_target_pairs={{8,0},{16,8},{24,16},{32,24},{40,32},{48,40},{56,48},{64,56},{72,6... | collective-permute-start | bytes 98312 | tf_op jit(solution)/shard_map/ppermute | solution.py:23
  149.5 12.5 %collective-permute-start.2 = (bf16[8,2048]{1,0:T(8,128)(2,1)S(1)}, bf16[8,2048]{1,0:T(8,128)(2,1)S(1)}, u32[]{:S(2)}, u32[]{:S(2)}) collective-permute-start(bf16[8,2048]{1,0:T(8,128)(2,1)S(1)} %bitcast.166), channel_id=1, source_target_pairs={{0,8},{8,16},{16,24},{24,32},{32,40},{40,48},{48,56},{56,64},{64,7... | collective-permute-start | bytes 98312 | tf_op jit(solution)/shard_map/ppermute | solution.py:21
  152.0 11.5 %collective-permute-start.4 = (bf16[4,32,128]{2,1,0:T(8,128)(2,1)S(1)}, bf16[4,32,128]{2,1,0:T(8,128)(2,1)S(1)}, u32[]{:S(2)}, u32[]{:S(2)}) collective-permute-start(bf16[4,32,128]{2,1,0:T(8,128)(2,1)S(1)} %get-tuple-element.80), channel_id=1, source_target_pairs={{0,1},{1,2},{2,3},{3,4},{4,5},{5,6},{6,7},{7,8},{8,9},{9,10},{10,1... | collective-permute-start | bytes 98312 | tf_op jit(solution)/shard_map/ppermute | solution.py:21
  154.0 9.5 %collective-permute-start.5 = (bf16[4,32,128]{2,1,0:T(8,128)(2,1)S(1)}, bf16[4,32,128]{2,1,0:T(8,128)(2,1)S(1)}, u32[]{:S(2)}, u32[]{:S(2)}) collective-permute-start(bf16[4,32,128]{2,1,0:T(8,128)(2,1)S(1)} %get-tuple-element.81), channel_id=1, source_target_pairs={{1,0},{2,1},{3,2},{4,3},{5,4},{6,5},{7,6},{8,7},{9,8},{10,9},{11,1... | collective-permute-start | bytes 98312 | tf_op jit(solution)/shard_map/ppermute | solution.py:23
  306.1 11.7 %copy-start.1 = (f32[32,96,64]{2,0,1:T(8,128)S(1)}, f32[32,96,64]{2,0,1:T(8,128)}, u32[]{:S(2)}) copy-start(f32[32,96,64]{2,0,1:T(8,128)} %fusion.37) | copy-start | bytes 2359300
  306.1 11.7 %copy-start.3 = (bf16[96,6]{1,0:T(8,128)(2,1)S(1)}, bf16[96,6]{1,0:T(8,128)(2,1)}, u32[]{:S(2)}) copy-start(bf16[96,6]{1,0:T(8,128)(2,1)} %fusion.49) | copy-start | bytes 3460
  306.1 11.7 %copy-start.6 = (pred[96,6]{1,0:T(8,128)(4,1)S(1)}, pred[96,6]{1,0:T(8,128)(4,1)}, u32[]{:S(2)}) copy-start(pred[96,6]{1,0:T(8,128)(4,1)} %copy.64) | copy-start | bytes 1732
where the time goes:
time: 331 us; the launch traced here: 328 us
  matrix products  94.2 us (28%)
  local copies, waits for them, and re-layouts  90.2 us (27%)
  blocking collectives  85.2 us (26%)
  starting transfers between devices  35.4 us (11%)
  other arithmetic  22.2 us (7%)
    dot_general x12, matrix products, near_block(): jnp.einsum('bmnj,bnrj->brm', kernel, values, preferred_element_type=wide)  70.5 us
    all_gather x1, blocking collectives, on_device(): lax.all_gather(group_sum.astype(narrow), 'gx', axis=0, tiled=True)  48 us
    ppermute x4, starting transfers between devices, padded(): lax.ppermute(head, axis, [((i + 1) % count, i) for i in range(ends)])  27.2 us
    unnamed x30, local copies, waits for them, and re-layouts  25.5 us
    psum x1, blocking collectives, on_device(): group_sum = lax.psum(mid_term, 'gy')  24.5 us
    gather x2, local copies, waits for them, and re-layouts, on_device(): jnp.take(coeff_rim, leaf_far - (first_leaf - leaves), axis=0)  15.6 us
    all_gather x1, blocking collectives, on_device(): siblings = lax.all_gather(mid_flat, 'gy', axis=0, tiled=True)  12.8 us
    dot_general x1, matrix products, on_device(): jnp.einsum('lkr,lkm->lrm', leaf_field, basis_out, preferred_element_type=...  10.3 us
  transfers between devices with their start and end apart: 8, of which 0 were waited for; matrix products, arithmetic and copies ran while one was open for 53% of the time, Pallas kernels for 0%

commit v1 on v0

--- a/solution.py
+++ b/solution.py
@@ -83,7 +83,7 @@
     mid_term = jnp.dot(cluster_up[0], mid_coeffs, preferred_element_type=wide).reshape(1, flat)
     mid_flat = mid_coeffs.reshape(1, flat)
     siblings = lax.all_gather(mid_flat, "gy", axis=0, tiled=True)
-    group_sum = lax.psum(mid_term, "gy")
+    group_sum = jnp.sum(lax.all_gather(mid_term, "gy"), axis=0)
     nearby = padded(siblings, (("gx", 0),), group_size)
     mid_picked = jnp.take(nearby, cluster_far[0] - (gx_index - 1) * group_size, axis=0)
     top_coeffs = lax.all_gather(group_sum.astype(narrow), "gx", axis=0, tiled=True)

time: 331 us -> 313 us (0.946)
  blocking collectives: 85.2 us -> 68.1 us
    psum x1 -> x0, blocking collectives: 24.5 us -> none  [on_device(): group_sum = lax.psum(mid_term, 'gy')]
    all_gather x0 -> x1, blocking collectives: none -> 12.8 us  [on_device(): group_sum = jnp.sum(lax.all_gather(mid_term, 'gy'), axis=0)]
    all_gather x1, blocking collectives: 48 us -> 42.5 us  [on_device(): lax.all_gather(group_sum.astype(narrow), 'gx', axis=0, tiled=True)]
  transfers between devices with their start and end apart: 8 -> 8, of which waited for: 0 -> 0; matrix products, arithmetic and copies ran while one was open for 53% -> 56% of each run, Pallas kernels for 0% -> 0%
where the time goes in v1:
time: 313 us; the launch traced here: 310 us
  matrix products  94.4 us (30%)
  local copies, waits for them, and re-layouts  89.9 us (29%)
  blocking collectives  68.1 us (22%)
  starting transfers between devices  34.9 us (11%)
  other arithmetic  21.5 us (7%)
    dot_general x12, matrix products, near_block(): jnp.einsum('bmnj,bnrj->brm', kernel, values, preferred_element_type=wide)  70.6 us
    all_gather x1, blocking collectives, on_device(): lax.all_gather(group_sum.astype(narrow), 'gx', axis=0, tiled=True)  42.5 us
    ppermute x4, starting transfers between devices, padded(): lax.ppermute(head, axis, [((i + 1) % count, i) for i in range(ends)])  27.2 us
    unnamed x30, local copies, waits for them, and re-layouts  25.4 us
    gather x2, local copies, waits for them, and re-layouts, on_device(): jnp.take(coeff_rim, leaf_far - (first_leaf - leaves), axis=0)  15.7 us
    all_gather x1, blocking collectives, on_device(): group_sum = jnp.sum(lax.all_gather(mid_term, 'gy'), axis=0)  12.8 us
    all_gather x1, blocking collectives, on_device(): siblings = lax.all_gather(mid_flat, 'gy', axis=0, tiled=True)  12.8 us
    dot_general x1, matrix products, on_device(): jnp.einsum('lkr,lkm->lrm', leaf_field, basis_out, preferred_element_type=...  10.3 us
  transfers between devices with their start and end apart: 8, of which 0 were waited for; matrix products, arithmetic and copies ran while one was open for 56% of the time, Pallas kernels for 0%

profile of v1, /device:TPU:8, one launch (start us, length us, event | category | flops | bytes accessed | tf_op | source)
XLA Modules:
  0.0 309.5 jit_solution(346814937421259603)
XLA Ops:
  0.0 2.6 convolution_convert_fusion
  2.6 1.3 copy.65
  4.0 1.0 copy.66
  5.0 9.3 %collective-permute-start.1 = (bf16[96,2048]{1,0:T(8,128)(2,1)}, bf16[96,2048]{1,0:T(8,128)(2,1)}, u32[]{:S(2)}, u32[]{:S(2)}) collective-permute-start(bf16[96,2048]{1,0:T(8,128)(2,1)} %copy.66), channel_id=1, source_target_pairs={{1,0},{2,1},{3,2},{4,3},{5,4},{6,5},{7,6},{8,7},{9,8},{10,9},{11,1... | collective-permute-start | bytes 1179656 | tf_op jit(solution)/shard_map/ppermute | solution.py:23
  14.2 1.9 collective-permute-start
  16.2 1.2 copy.80
  17.4 1.9 collective-permute-start.6
  19.4 8.0 %collective-permute-start.7 = (f32[4,7,128]{2,1,0:T(8,128)S(1)}, f32[4,7,128]{2,1,0:T(8,128)S(1)}, u32[]{:S(2)}, u32[]{:S(2)}) collective-permute-start(f32[4,7,128]{2,1,0:T(8,128)S(1)} %get-tuple-element.83), channel_id=1, source_target_pairs={{1,0},{2,1},{3,2},{4,3},{5,4},{6,5},{7,6},{8,7},{9,8},{10,9},{11,1... | collective-permute-start | bytes 43016 | tf_op jit(solution)/shard_map/ppermute | solution.py:23
  27.4 4.0 %copy.72 = bf16[96,64,64]{2,1,0:T(8,128)(2,1)} copy(bf16[96,64,64]{0,2,1:T(8,128)(2,1)} %param.26) | data formatting | bytes 1572864 | tf_op args[5]
  31.4 2.0 fusion.35
  33.6 12.8 %all-gather.1 = bf16[8,1,2048]{2,1,0:T(2,128)(2,1)S(1)} all-gather(bf16[1,1,2048]{2,1,0:T(2,128)(2,1)S(1)} %reshape.248), channel_id=1, replica_groups=mesh['gx'=32,'gy'=8] {'gy'}, dimensions={0}, use_global_device_ids=true | all-gather | bytes 36864 | tf_op jit(solution)/shard_map/all_gather | solution.py:85
  46.3 1.9 collective-permute-start.3
  48.4 0.8 fusion.62
  50.4 12.8 %all_gather.10 = f32[8,1,2048]{2,1,0:T(1,128)S(1)} all-gather(f32[1,1,2048]{2,1,0:T(1,128)S(1)} %all_gather_reshape.3), channel_id=1, replica_groups=mesh['gx'=32,'gy'=8] {'gy'}, dimensions={0}, use_global_device_ids=true | all-gather | bytes 73728 | tf_op jit(solution)/shard_map/all_gather | solution.py:86
  63.3 42.5 %all-gather = bf16[65536]{0:T(1024)(128)(2,1)S(1)} all-gather(bf16[2048]{0:T(1024)(128)(2,1)S(1)} %reduce_sum.18), channel_id=2, replica_groups=mesh['gx'=32,'gy'=8] {'gx'}, dimensions={0}, use_global_device_ids=true | all-gather | bytes 135168 | tf_op jit(solution)/shard_map/all_gather | solution.py:89
  107.1 1.1 convolution_bitcast_fusion.1
  108.3 1.8 fusion.33
  111.5 4.0 %copy.78 = bf16[96,64,64]{2,1,0:T(8,128)(2,1)} copy(bf16[96,64,64]{0,2,1:T(8,128)(2,1)} %param.27) | data formatting | bytes 1572864 | tf_op args[6]
  115.5 16.1 %copy.71 = bf16[96,6,64,64]{3,2,1,0:T(8,128)(2,1)} copy(bf16[96,6,64,64]{0,3,2,1:T(8,128)(2,1)} %param.28) | data formatting | bytes 9437184 | tf_op args[7]
  131.6 1.9 collective-permute-start.2
  133.5 1.9 collective-permute-start.4
  135.5 8.0 %collective-permute-start.5 = (bf16[4,32,128]{2,1,0:T(8,128)(2,1)S(1)}, bf16[4,32,128]{2,1,0:T(8,128)(2,1)S(1)}, u32[]{:S(2)}, u32[]{:S(2)}) collective-permute-start(bf16[4,32,128]{2,1,0:T(8,128)(2,1)S(1)} %get-tuple-element.81), channel_id=1, source_target_pairs={{1,0},{2,1},{3,2},{4,3},{5,4},{6,5},{7,6},{8,7},{9,8},{10,9},{11,1... | collective-permute-start | bytes 98312 | tf_op jit(solution)/shard_map/ppermute | solution.py:23
  145.0 1.2 pad_maximum_fusion.1
  146.2 130.7 %while.10 = (s32[]{:T(128)}, f32[12,8,32,128]{3,2,1,0:T(8,128)}, s32[12,8,8]{2,1,0:T(8,128)}, bf16[104,32,128]{2,1,0:T(8,128)(2,1)S(1)}, f32[104,7,128]{2,1,0:T(...) while((s32[]{:T(128)}, f32[12,8,32,128]{3,2,1,0:T(8,128)}, s32[12,8,8]{2,1,0:T(8,128)}, ...), condition=%wide.region_3.4_spmd, body=%wide.region_2.3_spmd.sunk | while | flops 87352896 | bytes 3410213 | solution.py:133
  147.7 0.8 dynamic-slice_bitcast_fusion.2
  149.8 0.8 fusion.83
  151.2 5.9 %fusion.84 = f32[12,8,32,128]{3,2,1,0:T(8,128)} fusion(f32[12,8,32,128]{3,2,1,0:T(8,128)} %get-tuple-element.149, s32[]{:T(128)S(6)} %copy.97, f32[8,8,128]{2,1,0:T(8,128)S(1)} %bitcast.156, f32[8,128]{1,0:T(8,128)} %get-tuple-element.132, f32[8,8,128]{2,1,0:T(8,128)S(1)} %bitcast.157, f32[8,8,128]{2,1,0:T(8,128)S(1)} %bitcast.158, ...), kind=kOutput, calls=%fused_computation.21.clone.1 | convolution fusion | flops 87293952 | bytes 897092 | tf_op jit(solution)/shard_map/while/body/eval_jaxpr/bmnj,bnrj->brm/dot_general | solution.py:131
  158.6 0.8 dynamic-slice_bitcast_fusion.2
  160.7 0.8 fusion.83
  162.1 5.9 %fusion.84 = f32[12,8,32,128]{3,2,1,0:T(8,128)} fusion(f32[12,8,32,128]{3,2,1,0:T(8,128)} %get-tuple-element.149, s32[]{:T(128)S(6)} %copy.97, f32[8,8,128]{2,1,0:T(8,128)S(1)} %bitcast.156, f32[8,128]{1,0:T(8,128)} %get-tuple-element.132, f32[8,8,128]{2,1,0:T(8,128)S(1)} %bitcast.157, f32[8,8,128]{2,1,0:T(8,128)S(1)} %bitcast.158, ...), kind=kOutput, calls=%fused_computation.21.clone.1 | convolution fusion | flops 87293952 | bytes 897092 | tf_op jit(solution)/shard_map/while/body/eval_jaxpr/bmnj,bnrj->brm/dot_general | solution.py:131
  169.5 0.8 dynamic-slice_bitcast_fusion.2
  171.6 0.8 fusion.83
  173.0 5.9 %fusion.84 = f32[12,8,32,128]{3,2,1,0:T(8,128)} fusion(f32[12,8,32,128]{3,2,1,0:T(8,128)} %get-tuple-element.149, s32[]{:T(128)S(6)} %copy.97, f32[8,8,128]{2,1,0:T(8,128)S(1)} %bitcast.156, f32[8,128]{1,0:T(8,128)} %get-tuple-element.132, f32[8,8,128]{2,1,0:T(8,128)S(1)} %bitcast.157, f32[8,8,128]{2,1,0:T(8,128)S(1)} %bitcast.158, ...), kind=kOutput, calls=%fused_computation.21.clone.1 | convolution fusion | flops 87293952 | bytes 897092 | tf_op jit(solution)/shard_map/while/body/eval_jaxpr/bmnj,bnrj->brm/dot_general | solution.py:131
  180.4 0.8 dynamic-slice_bitcast_fusion.2
  182.5 0.8 fusion.83
  183.9 5.9 %fusion.84 = f32[12,8,32,128]{3,2,1,0:T(8,128)} fusion(f32[12,8,32,128]{3,2,1,0:T(8,128)} %get-tuple-element.149, s32[]{:T(128)S(6)} %copy.97, f32[8,8,128]{2,1,0:T(8,128)S(1)} %bitcast.156, f32[8,128]{1,0:T(8,128)} %get-tuple-element.132, f32[8,8,128]{2,1,0:T(8,128)S(1)} %bitcast.157, f32[8,8,128]{2,1,0:T(8,128)S(1)} %bitcast.158, ...), kind=kOutput, calls=%fused_computation.21.clone.1 | convolution fusion | flops 87293952 | bytes 897092 | tf_op jit(solution)/shard_map/while/body/eval_jaxpr/bmnj,bnrj->brm/dot_general | solution.py:131
  191.2 0.8 dynamic-slice_bitcast_fusion.2
  193.4 0.8 fusion.83
  194.8 5.9 %fusion.84 = f32[12,8,32,128]{3,2,1,0:T(8,128)} fusion(f32[12,8,32,128]{3,2,1,0:T(8,128)} %get-tuple-element.149, s32[]{:T(128)S(6)} %copy.97, f32[8,8,128]{2,1,0:T(8,128)S(1)} %bitcast.156, f32[8,128]{1,0:T(8,128)} %get-tuple-element.132, f32[8,8,128]{2,1,0:T(8,128)S(1)} %bitcast.157, f32[8,8,128]{2,1,0:T(8,128)S(1)} %bitcast.158, ...), kind=kOutput, calls=%fused_computation.21.clone.1 | convolution fusion | flops 87293952 | bytes 897092 | tf_op jit(solution)/shard_map/while/body/eval_jaxpr/bmnj,bnrj->brm/dot_general | solution.py:131
  202.1 0.8 dynamic-slice_bitcast_fusion.2
  204.3 0.8 fusion.83
  205.7 5.9 %fusion.84 = f32[12,8,32,128]{3,2,1,0:T(8,128)} fusion(f32[12,8,32,128]{3,2,1,0:T(8,128)} %get-tuple-element.149, s32[]{:T(128)S(6)} %copy.97, f32[8,8,128]{2,1,0:T(8,128)S(1)} %bitcast.156, f32[8,128]{1,0:T(8,128)} %get-tuple-element.132, f32[8,8,128]{2,1,0:T(8,128)S(1)} %bitcast.157, f32[8,8,128]{2,1,0:T(8,128)S(1)} %bitcast.158, ...), kind=kOutput, calls=%fused_computation.21.clone.1 | convolution fusion | flops 87293952 | bytes 897092 | tf_op jit(solution)/shard_map/while/body/eval_jaxpr/bmnj,bnrj->brm/dot_general | solution.py:131
  213.0 0.8 dynamic-slice_bitcast_fusion.2
  215.2 0.8 fusion.83
  216.6 5.9 %fusion.84 = f32[12,8,32,128]{3,2,1,0:T(8,128)} fusion(f32[12,8,32,128]{3,2,1,0:T(8,128)} %get-tuple-element.149, s32[]{:T(128)S(6)} %copy.97, f32[8,8,128]{2,1,0:T(8,128)S(1)} %bitcast.156, f32[8,128]{1,0:T(8,128)} %get-tuple-element.132, f32[8,8,128]{2,1,0:T(8,128)S(1)} %bitcast.157, f32[8,8,128]{2,1,0:T(8,128)S(1)} %bitcast.158, ...), kind=kOutput, calls=%fused_computation.21.clone.1 | convolution fusion | flops 87293952 | bytes 897092 | tf_op jit(solution)/shard_map/while/body/eval_jaxpr/bmnj,bnrj->brm/dot_general | solution.py:131
  223.9 0.8 dynamic-slice_bitcast_fusion.2
  226.1 0.8 fusion.83
  227.5 5.9 %fusion.84 = f32[12,8,32,128]{3,2,1,0:T(8,128)} fusion(f32[12,8,32,128]{3,2,1,0:T(8,128)} %get-tuple-element.149, s32[]{:T(128)S(6)} %copy.97, f32[8,8,128]{2,1,0:T(8,128)S(1)} %bitcast.156, f32[8,128]{1,0:T(8,128)} %get-tuple-element.132, f32[8,8,128]{2,1,0:T(8,128)S(1)} %bitcast.157, f32[8,8,128]{2,1,0:T(8,128)S(1)} %bitcast.158, ...), kind=kOutput, calls=%fused_computation.21.clone.1 | convolution fusion | flops 87293952 | bytes 897092 | tf_op jit(solution)/shard_map/while/body/eval_jaxpr/bmnj,bnrj->brm/dot_general | solution.py:131
  234.8 0.8 dynamic-slice_bitcast_fusion.2
  237.0 0.8 fusion.83
  238.4 5.9 %fusion.84 = f32[12,8,32,128]{3,2,1,0:T(8,128)} fusion(f32[12,8,32,128]{3,2,1,0:T(8,128)} %get-tuple-element.149, s32[]{:T(128)S(6)} %copy.97, f32[8,8,128]{2,1,0:T(8,128)S(1)} %bitcast.156, f32[8,128]{1,0:T(8,128)} %get-tuple-element.132, f32[8,8,128]{2,1,0:T(8,128)S(1)} %bitcast.157, f32[8,8,128]{2,1,0:T(8,128)S(1)} %bitcast.158, ...), kind=kOutput, calls=%fused_computation.21.clone.1 | convolution fusion | flops 87293952 | bytes 897092 | tf_op jit(solution)/shard_map/while/body/eval_jaxpr/bmnj,bnrj->brm/dot_general | solution.py:131
  245.7 0.8 dynamic-slice_bitcast_fusion.2
  247.8 0.8 fusion.83
  249.3 5.9 %fusion.84 = f32[12,8,32,128]{3,2,1,0:T(8,128)} fusion(f32[12,8,32,128]{3,2,1,0:T(8,128)} %get-tuple-element.149, s32[]{:T(128)S(6)} %copy.97, f32[8,8,128]{2,1,0:T(8,128)S(1)} %bitcast.156, f32[8,128]{1,0:T(8,128)} %get-tuple-element.132, f32[8,8,128]{2,1,0:T(8,128)S(1)} %bitcast.157, f32[8,8,128]{2,1,0:T(8,128)S(1)} %bitcast.158, ...), kind=kOutput, calls=%fused_computation.21.clone.1 | convolution fusion | flops 87293952 | bytes 897092 | tf_op jit(solution)/shard_map/while/body/eval_jaxpr/bmnj,bnrj->brm/dot_general | solution.py:131
  258.7 0.8 fusion.83
  260.2 5.9 %fusion.84 = f32[12,8,32,128]{3,2,1,0:T(8,128)} fusion(f32[12,8,32,128]{3,2,1,0:T(8,128)} %get-tuple-element.149, s32[]{:T(128)S(6)} %copy.97, f32[8,8,128]{2,1,0:T(8,128)S(1)} %bitcast.156, f32[8,128]{1,0:T(8,128)} %get-tuple-element.132, f32[8,8,128]{2,1,0:T(8,128)S(1)} %bitcast.157, f32[8,8,128]{2,1,0:T(8,128)S(1)} %bitcast.158, ...), kind=kOutput, calls=%fused_computation.21.clone.1 | convolution fusion | flops 87293952 | bytes 897092 | tf_op jit(solution)/shard_map/while/body/eval_jaxpr/bmnj,bnrj->brm/dot_general | solution.py:131
  269.6 0.8 fusion.83
  271.0 5.9 %fusion.84 = f32[12,8,32,128]{3,2,1,0:T(8,128)} fusion(f32[12,8,32,128]{3,2,1,0:T(8,128)} %get-tuple-element.149, s32[]{:T(128)S(6)} %copy.97, f32[8,8,128]{2,1,0:T(8,128)S(1)} %bitcast.156, f32[8,128]{1,0:T(8,128)} %get-tuple-element.132, f32[8,8,128]{2,1,0:T(8,128)S(1)} %bitcast.157, f32[8,8,128]{2,1,0:T(8,128)S(1)} %bitcast.158, ...), kind=kOutput, calls=%fused_computation.21.clone.1 | convolution fusion | flops 87293952 | bytes 897092 | tf_op jit(solution)/shard_map/while/body/eval_jaxpr/bmnj,bnrj->brm/dot_general | solution.py:131
  276.9 1.1 convolution_bitcast_fusion.3
  278.0 4.2 %fusion.37 = f32[32,96,64]{2,0,1:T(8,128)} fusion(bf16[96,64,64]{2,1,0:T(8,128)(2,1)} %copy.78, f32[32,64]{1,0:T(8,128)S(1)} %convolution_bitcast_fusion.3, bf16[32,64]{1,0:T(8,128)(2,1)} %fusion.33, bf16[1,64,64]{2,1,0:T(8,128)(2,1)} %param.32), kind=kOutput, calls=%fused_computation.60 | convolution fusion | flops 25432064 | bytes 1593344 | tf_op jit(solution)/shard_map/lik,kr->lir/dot_general | solution.py:119
  282.3 1.3 pad_maximum_fusion
  283.6 4.0 %gather_fusion.2 = bf16[576,2048]{1,0:T(8,128)(2,1)} fusion(bf16[288,2048]{1,0:T(8,128)(2,1)S(1)} %pad_maximum_fusion, s32[1024]{0:T(1024)S(1)} %pad_clamp_fusion.3), kind=kCustom, calls=%fused_computation.2 | custom fusion | bytes 4720896 | tf_op jit(solution)/shard_map/jit(_take)/gather | solution.py:110
  287.6 11.7 %gather.23 = bf16[96,6,64,32]{3,2,1,0:T(8,128)(2,1)} reshape(bf16[576,2048]{1,0:T(8,128)(2,1)} %gather_fusion.2) | data formatting | bytes 4718592 | tf_op jit(solution)/shard_map/jit(_take)/gather | solution.py:110
  299.3 10.3 %bitcast_add_fusion.1 = f32[96,32,128]{2,1,0:T(8,128)} fusion(f32[12,8,32,128]{3,2,1,0:T(8,128)} %get-tuple-element.37, bf16[96,64,128]{2,1,0:T(8,128)(2,1)S(1)} %copy-done, f32[32,96,64]{2,0,1:T(8,128)S(1)} %copy-done.1, bf16[96,6,64,64]{3,2,1,0:T(8,128)(2,1)} %copy.71, bf16[96,6,64,32]{3,2,1,0:T(8,128)(2,1)} %gather.23, pred[96,6]{1,0:T(8,128)(4,1)S(1)} %copy-done.6, ...), kind=kOutput, calls=%fused_computation.44 | convolution fusion | flops 204472320 | bytes 12584640 | tf_op jit(solution)/shard_map/lkr,lkm->lrm/dot_general | solution.py:121
  (161 shorter events, 48.8 us)
Async XLA Ops:
  0.0 299.3 %copy-start = (bf16[96,64,128]{2,1,0:T(8,128)(2,1)S(1)}, bf16[96,64,128]{2,1,0:T(8,128)(2,1)}, u32[]{:S(2)}) copy-start(bf16[96,64,128]{2,1,0:T(8,128)(2,1)} %param.25) | copy-start | bytes 4718596
  5.0 277.3 %collective-permute-start.1 = (bf16[96,2048]{1,0:T(8,128)(2,1)}, bf16[96,2048]{1,0:T(8,128)(2,1)}, u32[]{:S(2)}, u32[]{:S(2)}) collective-permute-start(bf16[96,2048]{1,0:T(8,128)(2,1)} %copy.66), channel_id=1, source_target_pairs={{1,0},{2,1},{3,2},{4,3},{5,4},{6,5},{7,6},{8,7},{9,8},{10,9},{11,1... | collective-permute-start | bytes 1179656 | tf_op jit(solution)/shard_map/ppermute | solution.py:23
  14.2 268.0 %collective-permute-start = (bf16[96,2048]{1,0:T(8,128)(2,1)}, bf16[96,2048]{1,0:T(8,128)(2,1)}, u32[]{:S(2)}, u32[]{:S(2)}) collective-permute-start(bf16[96,2048]{1,0:T(8,128)(2,1)} %copy.66), channel_id=1, source_target_pairs={{0,1},{1,2},{2,3},{3,4},{4,5},{5,6},{6,7},{7,8},{8,9},{9,10},{10,1... | collective-permute-start | bytes 1179656 | tf_op jit(solution)/shard_map/ppermute | solution.py:21
  17.4 114.2 %collective-permute-start.6 = (f32[4,7,128]{2,1,0:T(8,128)S(1)}, f32[4,7,128]{2,1,0:T(8,128)S(1)}, u32[]{:S(2)}, u32[]{:S(2)}) collective-permute-start(f32[4,7,128]{2,1,0:T(8,128)S(1)} %get-tuple-element.82), channel_id=1, source_target_pairs={{0,1},{1,2},{2,3},{3,4},{4,5},{5,6},{6,7},{7,8},{8,9},{9,10},{10,1... | collective-permute-start | bytes 43016 | tf_op jit(solution)/shard_map/ppermute | solution.py:21
  19.3 29.0 %copy-start.10 = (s32[1,6]{1,0:T(1,128)S(1)}, s32[1,6]{1,0:T(1,128)}, u32[]{:S(2)}) copy-start(s32[1,6]{1,0:T(1,128)} %param.34) | copy-start | bytes 76
  19.3 29.0 %copy-start.11 = (s32[1,6]{1,0:T(1,128)S(1)}, s32[1,6]{1,0:T(1,128)}, u32[]{:S(2)}) copy-start(s32[1,6]{1,0:T(1,128)} %param.38) | copy-start | bytes 76
  19.3 29.9 %copy-start.9 = (s32[96]{0:T(128)S(1)}, s32[96]{0:T(128)}, u32[]{:S(2)}) copy-start(s32[96]{0:T(128)} %param.30) | copy-start | bytes 1156
  19.3 30.5 %copy-start.7 = (s32[96,6]{0,1:T(8,128)S(1)}, s32[96,6]{0,1:T(8,128)}, u32[]{:S(2)}) copy-start(s32[96,6]{0,1:T(8,128)} %param.29) | copy-start | bytes 6916
  19.3 30.8 %copy-start.4 = (bf16[1,64,64]{2,1,0:T(8,128)(2,1)S(1)}, bf16[1,64,64]{2,1,0:T(8,128)(2,1)}, u32[]{:S(2)}) copy-start(bf16[1,64,64]{2,1,0:T(8,128)(2,1)} %param.31) | copy-start | bytes 24580
  19.4 114.1 %collective-permute-start.7 = (f32[4,7,128]{2,1,0:T(8,128)S(1)}, f32[4,7,128]{2,1,0:T(8,128)S(1)}, u32[]{:S(2)}, u32[]{:S(2)}) collective-permute-start(f32[4,7,128]{2,1,0:T(8,128)S(1)} %get-tuple-element.83), channel_id=1, source_target_pairs={{1,0},{2,1},{3,2},{4,3},{5,4},{6,5},{7,6},{8,7},{9,8},{10,9},{11,1... | collective-permute-start | bytes 43016 | tf_op jit(solution)/shard_map/ppermute | solution.py:23
  31.4 74.7 %copy-start.2 = (bf16[32,64,64]{2,1,0:T(8,128)(2,1)S(1)}, bf16[32,64,64]{2,1,0:T(8,128)(2,1)}, u32[]{:S(2)}) copy-start(bf16[32,64,64]{2,1,0:T(8,128)(2,1)} %param.35) | copy-start | bytes 786436
  31.4 75.7 %copy-start.8 = (s32[96,8]{0,1:T(8,128)S(1)}, s32[96,8]{0,1:T(8,128)}, u32[]{:S(2)}) copy-start(s32[96,8]{0,1:T(8,128)} %param.23) | copy-start | bytes 9220
  31.4 76.9 %copy-start.5 = (bf16[1,64,64]{2,1,0:T(8,128)(2,1)S(1)}, bf16[1,64,64]{2,1,0:T(8,128)(2,1)}, u32[]{:S(2)}) copy-start(bf16[1,64,64]{2,1,0:T(8,128)(2,1)} %param.36) | copy-start | bytes 24580
  46.3 89.1 %collective-permute-start.3 = (bf16[8,2048]{1,0:T(8,128)(2,1)S(1)}, bf16[8,2048]{1,0:T(8,128)(2,1)S(1)}, u32[]{:S(2)}, u32[]{:S(2)}) collective-permute-start(bf16[8,2048]{1,0:T(8,128)(2,1)S(1)} %bitcast.162), channel_id=1, source_target_pairs={{8,0},{16,8},{24,16},{32,24},{40,32},{48,40},{56,48},{64,56},{72,6... | collective-permute-start | bytes 98312 | tf_op jit(solution)/shard_map/ppermute | solution.py:23
  131.6 12.0 %collective-permute-start.2 = (bf16[8,2048]{1,0:T(8,128)(2,1)S(1)}, bf16[8,2048]{1,0:T(8,128)(2,1)S(1)}, u32[]{:S(2)}, u32[]{:S(2)}) collective-permute-start(bf16[8,2048]{1,0:T(8,128)(2,1)S(1)} %bitcast.163), channel_id=1, source_target_pairs={{0,8},{8,16},{16,24},{24,32},{32,40},{40,48},{48,56},{56,64},{64,7... | collective-permute-start | bytes 98312 | tf_op jit(solution)/shard_map/ppermute | solution.py:21
  133.5 11.5 %collective-permute-start.4 = (bf16[4,32,128]{2,1,0:T(8,128)(2,1)S(1)}, bf16[4,32,128]{2,1,0:T(8,128)(2,1)S(1)}, u32[]{:S(2)}, u32[]{:S(2)}) collective-permute-start(bf16[4,32,128]{2,1,0:T(8,128)(2,1)S(1)} %get-tuple-element.80), channel_id=1, source_target_pairs={{0,1},{1,2},{2,3},{3,4},{4,5},{5,6},{6,7},{7,8},{8,9},{9,10},{10,1... | collective-permute-start | bytes 98312 | tf_op jit(solution)/shard_map/ppermute | solution.py:21
  135.5 9.5 %collective-permute-start.5 = (bf16[4,32,128]{2,1,0:T(8,128)(2,1)S(1)}, bf16[4,32,128]{2,1,0:T(8,128)(2,1)S(1)}, u32[]{:S(2)}, u32[]{:S(2)}) collective-permute-start(bf16[4,32,128]{2,1,0:T(8,128)(2,1)S(1)} %get-tuple-element.81), channel_id=1, source_target_pairs={{1,0},{2,1},{3,2},{4,3},{5,4},{6,5},{7,6},{8,7},{9,8},{10,9},{11,1... | collective-permute-start | bytes 98312 | tf_op jit(solution)/shard_map/ppermute | solution.py:23
  287.6 11.7 %copy-start.1 = (f32[32,96,64]{2,0,1:T(8,128)S(1)}, f32[32,96,64]{2,0,1:T(8,128)}, u32[]{:S(2)}) copy-start(f32[32,96,64]{2,0,1:T(8,128)} %fusion.37) | copy-start | bytes 2359300
  287.6 11.7 %copy-start.3 = (bf16[96,6]{1,0:T(8,128)(2,1)S(1)}, bf16[96,6]{1,0:T(8,128)(2,1)}, u32[]{:S(2)}) copy-start(bf16[96,6]{1,0:T(8,128)(2,1)} %fusion.49) | copy-start | bytes 3460
  287.6 11.7 %copy-start.6 = (pred[96,6]{1,0:T(8,128)(4,1)S(1)}, pred[96,6]{1,0:T(8,128)(4,1)}, u32[]{:S(2)}) copy-start(pred[96,6]{1,0:T(8,128)(4,1)} %copy.64) | copy-start | bytes 1732
